TPU v7x, 256 devices: a whole 4x4x8 slice. The times are simulated.
256 devices in a mesh: tile: 128 (over z, x_hi, y, core), real: 2 (over x_lo).
Axes of the slice: x: 4 (x_hi: 2, x_lo: 2; x = x_hi * 2 + x_lo), y: 4, z: 8, core: 2. Of those that a mesh axis runs over, the one named last changes fastest.
Arguments:
- voltage: float32 [64, 131072], P('real', 'tile'), parts along dimension 0, may hold values from -4 to 4
- recovery: float32 [64, 131072], P('real', 'tile'), parts along dimension 0, may hold values from -3 to 3
- increments: float32 [10, 64, 131072], P(None, 'real', 'tile'), parts along dimension 1, may hold values from -6 to 6
- band_weight: bfloat16 [131072, 3072], P('tile'), may hold values from -0.125 to 0.125
- time_scale: float32 [131072], P('tile'), may hold values from 0.05 to 0.5
- tract_in: bfloat16 [4, 131072, 256], P(None, 'tile'), may hold values from -0.375 to 0.375
- tract_out: bfloat16 [4, 131072, 256], P(None, 'tile'), may hold values from -0.1875 to 0.1875
- matching_masks: int32 [4], replicated, may hold values from 1 to 127, as said below
- tract_on: int32 [128, 4], P('tile'), may hold values 0 or 1
Outputs:
- voltage_end: float32 [64, 131072], P('real', 'tile'), parts along dimension 0
- recovery_end: float32 [64, 131072], P('real', 'tile'), parts along dimension 0
There are 2 independent parts, one for each index of `real`. A program takes and returns all parts, laid end to end along the dimension named above; an argument that names none is the same for every part. Nothing has to cross between parts.
Inputs may be any that keep to these rules, and one draw needn't show every extreme that they name: `matching_masks`: the 4 masks are distinct.
All inputs are finite; a program needn't handle non-finite values. No bound on the sum of `tract_on` on one device may be relied on, other than what follows from the above.
Results may differ from a plain program's by a relative error of at most 0.0013.
Values may be sent and summed in bfloat16 or wider, within the bound.
No kernel may reach another device: no remote copies, remote signals or barrier semaphores. Data moves between devices by JAX's collectives and lax.ppermute only.
A program may use at most 64 MiB of HBM per device.

v0:
```python
import math

import jax
import jax.numpy as jnp
from jax import lax
from jax.sharding import PartitionSpec as P

TILE_V = 1024
HW = 1024


time_step = 0.1
noise_gain = 0.5
shift_a = 0.7
damp_b = 0.8
drive_level = 0.5
band_gain = 1.0
tract_gain = 0.5


def padded_2(cells, sides, width):
    for axis, dim in sides:
        count = lax.axis_size(axis)
        ends = count - 1
        head = lax.slice_in_dim(cells, 0, width, axis=dim)
        tail = lax.slice_in_dim(cells, cells.shape[dim] - width, cells.shape[dim], axis=dim)
        cells = jnp.concatenate(
            [
                lax.ppermute(tail, axis, [(i, (i + 1) % count) for i in range(ends)]),
                cells,
                lax.ppermute(head, axis, [((i + 1) % count, i) for i in range(ends)]),
            ],
            axis=dim,
        )
    return cells


def swapped(block, axis, apart):
    count = lax.axis_size(axis)
    route = []
    for low in range(count):
        high = low | 1 << apart
        if high != low and high < count:
            route += [(low, high), (high, low)]
    return lax.ppermute(block, axis, route)


def contract_last(left, right):
    return lax.dot_general(
        left, right, (((1,), (1,)), ((), ())), preferred_element_type=jnp.float32
    )


def per_device(
    voltage,
    recovery,
    increments,
    band_weight,
    time_scale,
    tract_in,
    tract_out,
    matching_masks,
    tract_on,
):
    window_width = TILE_V + 2 * HW
    row_index = jnp.arange(TILE_V, dtype=jnp.int32)[:, None]
    col_index = jnp.arange(window_width, dtype=jnp.int32)[None, :]
    inband = (col_index - row_index >= 0) & (col_index - row_index <= 2 * HW)
    banded = jnp.where(inband, band_weight, jnp.zeros((), jnp.bfloat16))
    tile_count = lax.axis_size("tile")
    bit_count = tile_count.bit_length() - 1
    bit_sequence = list(range(bit_count))
    tract_gate = tract_on[0].astype(jnp.bfloat16)

    def advance(step_index, state_pair):
        voltage_now, recovery_now = state_pair
        rounded = voltage_now.astype(jnp.bfloat16)
        padded = padded_2(rounded, (("tile", 1),), HW)
        band_drive = contract_last(padded, banded)
        projected = jnp.einsum(
            "rv,mvk->mrk", rounded, tract_out, preferred_element_type=jnp.float32
        ).astype(jnp.bfloat16)
        for bit in bit_sequence:
            arrived = swapped(projected, "tile", bit)
            chosen = jnp.bitwise_and(jnp.right_shift(matching_masks, bit), 1) == 1
            projected = jnp.where(chosen[:, None, None], arrived, projected)
        received = projected * tract_gate[:, None, None]
        tract_drive = jnp.einsum(
            "mrk,mvk->rv", received, tract_in, preferred_element_type=jnp.float32
        )
        kick_now = lax.dynamic_index_in_dim(increments, step_index, 0, keepdims=False)
        total_drive = band_gain * band_drive + tract_gain * tract_drive + drive_level
        voltage_new = (
            voltage_now
            + time_step * (voltage_now - voltage_now**3 / 3.0 - recovery_now + total_drive)
            + noise_gain * math.sqrt(time_step) * kick_now
        )
        recovery_new = recovery_now + time_step * time_scale[None, :] * (
            voltage_now + shift_a - damp_b * recovery_now
        )
        return (voltage_new, recovery_new)

    voltage_end, recovery_end = lax.fori_loop(0, increments.shape[0], advance, (voltage, recovery))
    return (voltage_end, recovery_end)


def solution(mesh):
    placed = (
        P("real", "tile"),
        P("real", "tile"),
        P(None, "real", "tile"),
        P("tile", None),
        P("tile"),
        P(None, "tile", None),
        P(None, "tile", None),
        P(),
        P("tile", None),
    )
    return jax.shard_map(
        per_device,
        mesh=mesh,
        in_specs=placed,
        out_specs=(P("real", "tile"), P("real", "tile")),
        check_vma=False,
    )
```

profile of v0, /device:TPU:32, one launch (start us, length us, event | category | flops | bytes accessed | tf_op | source)
XLA Modules:
  0.0 495.4 jit_solution(3703797818611038316)
XLA Ops:
  0.7 6.4 %fusion.24 = bf16[1024,3072]{1,0:T(8,128)(2,1)} fusion(bf16[1024,3072]{1,0:T(8,128)(2,1)} %param.14), kind=kLoop, calls=%fused_computation.44 | loop fusion | flops 15728640 | bytes 12582912 | tf_op jit(solution)/shard_map/jit(_where)/select_n | solution.py:69
  7.1 487.6 %while.15 = (s32[]{:T(128)}, f32[32,1024]{1,0:T(8,128)S(1)}, f32[32,1024]{1,0:T(8,128)S(1)}, bf16[1024,3072]{1,0:T(8,128)(2,1)}, s32[4]{0:T(128)S(1)}, /*index=5...) while((s32[]{:T(128)}, f32[32,1024]{1,0:T(8,128)S(1)}, ...), condition=%wide.region_1.2_spmd, body=%wide.region_0.1_spmd.sunk | while | flops 337052736 | bytes 16003633 | solution.py:103
  36.0 5.6 %collective-permute-start.6 = (bf16[4,32,256]{2,1,0:T(8,128)(2,1)S(1)}, bf16[4,32,256]{2,1,0:T(8,128)(2,1)S(1)}, u32[]{:S(2)}, u32[]{:S(2)}) collective-permute-start(bf16[4,32,256]{2,1,0:T(8,128)(2,1)S(1)} %broadcast_select_fusion.17), channel_id=1, source_target_pairs={{0,128},{128,0},{2,130},{130,2},{4,132},{132,4},{6,134},{134,6},{8... | collective-permute-start | bytes 196616 | tf_op jit(solution)/shard_map/while/body/eval_jaxpr/ppermute | solution.py:45
  48.2 6.1 %collective-permute-done.8 = bf16[32,1024]{1,0:T(8,128)(2,1)S(1)} collective-permute-done((bf16[32,1024]{1,0:T(8,128)(2,1)S(1)}, bf16[32,1024]{1,0:T(8,128)(2,1)S(1)}, u32[]{:S(2)}, u32[]{:S(2)}) %collective-permute-start.8) | collective-permute-done | bytes 65568 | tf_op jit(solution)/shard_map/while/body/eval_jaxpr/ppermute | solution.py:29
  54.4 4.8 fusion.45
  65.5 5.8 %collective-permute-done.2 = bf16[4,32,256]{2,1,0:T(8,128)(2,1)S(1)} collective-permute-done((bf16[4,32,256]{2,1,0:T(8,128)(2,1)S(1)}, bf16[4,32,256]{2,1,0:T(8,128)(2,1)S(1)}, u32[]{:S(2)}, u32[]{:S(2)}) %collective-permute-start.2) | collective-permute-done | bytes 65568 | tf_op jit(solution)/shard_map/while/body/eval_jaxpr/ppermute | solution.py:45
  113.5 5.8 %collective-permute-done.2 = bf16[4,32,256]{2,1,0:T(8,128)(2,1)S(1)} collective-permute-done((bf16[4,32,256]{2,1,0:T(8,128)(2,1)S(1)}, bf16[4,32,256]{2,1,0:T(8,128)(2,1)S(1)}, u32[]{:S(2)}, u32[]{:S(2)}) %collective-permute-start.2) | collective-permute-done | bytes 65568 | tf_op jit(solution)/shard_map/while/body/eval_jaxpr/ppermute | solution.py:45
  119.4 5.8 %collective-permute-done.3 = bf16[4,32,256]{2,1,0:T(8,128)(2,1)S(1)} collective-permute-done((bf16[4,32,256]{2,1,0:T(8,128)(2,1)S(1)}, bf16[4,32,256]{2,1,0:T(8,128)(2,1)S(1)}, u32[]{:S(2)}, u32[]{:S(2)}) %collective-permute-start.3) | collective-permute-done | bytes 65568 | tf_op jit(solution)/shard_map/while/body/eval_jaxpr/ppermute | solution.py:45
  162.2 5.8 %collective-permute-done.2 = bf16[4,32,256]{2,1,0:T(8,128)(2,1)S(1)} collective-permute-done((bf16[4,32,256]{2,1,0:T(8,128)(2,1)S(1)}, bf16[4,32,256]{2,1,0:T(8,128)(2,1)S(1)}, u32[]{:S(2)}, u32[]{:S(2)}) %collective-permute-start.2) | collective-permute-done | bytes 65568 | tf_op jit(solution)/shard_map/while/body/eval_jaxpr/ppermute | solution.py:45
  168.1 5.8 %collective-permute-done.3 = bf16[4,32,256]{2,1,0:T(8,128)(2,1)S(1)} collective-permute-done((bf16[4,32,256]{2,1,0:T(8,128)(2,1)S(1)}, bf16[4,32,256]{2,1,0:T(8,128)(2,1)S(1)}, u32[]{:S(2)}, u32[]{:S(2)}) %collective-permute-start.3) | collective-permute-done | bytes 65568 | tf_op jit(solution)/shard_map/while/body/eval_jaxpr/ppermute | solution.py:45
  198.1 4.8 fusion.45
  209.2 5.8 %collective-permute-done.2 = bf16[4,32,256]{2,1,0:T(8,128)(2,1)S(1)} collective-permute-done((bf16[4,32,256]{2,1,0:T(8,128)(2,1)S(1)}, bf16[4,32,256]{2,1,0:T(8,128)(2,1)S(1)}, u32[]{:S(2)}, u32[]{:S(2)}) %collective-permute-start.2) | collective-permute-done | bytes 65568 | tf_op jit(solution)/shard_map/while/body/eval_jaxpr/ppermute | solution.py:45
  215.1 5.8 %collective-permute-done.3 = bf16[4,32,256]{2,1,0:T(8,128)(2,1)S(1)} collective-permute-done((bf16[4,32,256]{2,1,0:T(8,128)(2,1)S(1)}, bf16[4,32,256]{2,1,0:T(8,128)(2,1)S(1)}, u32[]{:S(2)}, u32[]{:S(2)}) %collective-permute-start.3) | collective-permute-done | bytes 65568 | tf_op jit(solution)/shard_map/while/body/eval_jaxpr/ppermute | solution.py:45
  221.0 4.9 collective-permute-done.4
  242.4 5.3 %collective-permute-done.8 = bf16[32,1024]{1,0:T(8,128)(2,1)S(1)} collective-permute-done((bf16[32,1024]{1,0:T(8,128)(2,1)S(1)}, bf16[32,1024]{1,0:T(8,128)(2,1)S(1)}, u32[]{:S(2)}, u32[]{:S(2)}) %collective-permute-start.8) | collective-permute-done | bytes 65568 | tf_op jit(solution)/shard_map/while/body/eval_jaxpr/ppermute | solution.py:29
  258.9 5.8 %collective-permute-done.2 = bf16[4,32,256]{2,1,0:T(8,128)(2,1)S(1)} collective-permute-done((bf16[4,32,256]{2,1,0:T(8,128)(2,1)S(1)}, bf16[4,32,256]{2,1,0:T(8,128)(2,1)S(1)}, u32[]{:S(2)}, u32[]{:S(2)}) %collective-permute-start.2) | collective-permute-done | bytes 65568 | tf_op jit(solution)/shard_map/while/body/eval_jaxpr/ppermute | solution.py:45
  264.7 5.8 %collective-permute-done.3 = bf16[4,32,256]{2,1,0:T(8,128)(2,1)S(1)} collective-permute-done((bf16[4,32,256]{2,1,0:T(8,128)(2,1)S(1)}, bf16[4,32,256]{2,1,0:T(8,128)(2,1)S(1)}, u32[]{:S(2)}, u32[]{:S(2)}) %collective-permute-start.3) | collective-permute-done | bytes 65568 | tf_op jit(solution)/shard_map/while/body/eval_jaxpr/ppermute | solution.py:45
  270.6 4.9 collective-permute-done.4
  294.9 4.8 fusion.45
  306.0 5.8 %collective-permute-done.2 = bf16[4,32,256]{2,1,0:T(8,128)(2,1)S(1)} collective-permute-done((bf16[4,32,256]{2,1,0:T(8,128)(2,1)S(1)}, bf16[4,32,256]{2,1,0:T(8,128)(2,1)S(1)}, u32[]{:S(2)}, u32[]{:S(2)}) %collective-permute-start.2) | collective-permute-done | bytes 65568 | tf_op jit(solution)/shard_map/while/body/eval_jaxpr/ppermute | solution.py:45
  311.9 5.8 %collective-permute-done.3 = bf16[4,32,256]{2,1,0:T(8,128)(2,1)S(1)} collective-permute-done((bf16[4,32,256]{2,1,0:T(8,128)(2,1)S(1)}, bf16[4,32,256]{2,1,0:T(8,128)(2,1)S(1)}, u32[]{:S(2)}, u32[]{:S(2)}) %collective-permute-start.3) | collective-permute-done | bytes 65568 | tf_op jit(solution)/shard_map/while/body/eval_jaxpr/ppermute | solution.py:45
  355.6 5.8 %collective-permute-done.2 = bf16[4,32,256]{2,1,0:T(8,128)(2,1)S(1)} collective-permute-done((bf16[4,32,256]{2,1,0:T(8,128)(2,1)S(1)}, bf16[4,32,256]{2,1,0:T(8,128)(2,1)S(1)}, u32[]{:S(2)}, u32[]{:S(2)}) %collective-permute-start.2) | collective-permute-done | bytes 65568 | tf_op jit(solution)/shard_map/while/body/eval_jaxpr/ppermute | solution.py:45
  361.4 5.8 %collective-permute-done.3 = bf16[4,32,256]{2,1,0:T(8,128)(2,1)S(1)} collective-permute-done((bf16[4,32,256]{2,1,0:T(8,128)(2,1)S(1)}, bf16[4,32,256]{2,1,0:T(8,128)(2,1)S(1)}, u32[]{:S(2)}, u32[]{:S(2)}) %collective-permute-start.3) | collective-permute-done | bytes 65568 | tf_op jit(solution)/shard_map/while/body/eval_jaxpr/ppermute | solution.py:45
  367.3 4.9 collective-permute-done.4
  388.2 5.2 %collective-permute-done.8 = bf16[32,1024]{1,0:T(8,128)(2,1)S(1)} collective-permute-done((bf16[32,1024]{1,0:T(8,128)(2,1)S(1)}, bf16[32,1024]{1,0:T(8,128)(2,1)S(1)}, u32[]{:S(2)}, u32[]{:S(2)}) %collective-permute-start.8) | collective-permute-done | bytes 65568 | tf_op jit(solution)/shard_map/while/body/eval_jaxpr/ppermute | solution.py:29
  393.3 4.8 fusion.45
  404.5 5.8 %collective-permute-done.2 = bf16[4,32,256]{2,1,0:T(8,128)(2,1)S(1)} collective-permute-done((bf16[4,32,256]{2,1,0:T(8,128)(2,1)S(1)}, bf16[4,32,256]{2,1,0:T(8,128)(2,1)S(1)}, u32[]{:S(2)}, u32[]{:S(2)}) %collective-permute-start.2) | collective-permute-done | bytes 65568 | tf_op jit(solution)/shard_map/while/body/eval_jaxpr/ppermute | solution.py:45
  410.4 5.8 %collective-permute-done.3 = bf16[4,32,256]{2,1,0:T(8,128)(2,1)S(1)} collective-permute-done((bf16[4,32,256]{2,1,0:T(8,128)(2,1)S(1)}, bf16[4,32,256]{2,1,0:T(8,128)(2,1)S(1)}, u32[]{:S(2)}, u32[]{:S(2)}) %collective-permute-start.3) | collective-permute-done | bytes 65568 | tf_op jit(solution)/shard_map/while/body/eval_jaxpr/ppermute | solution.py:45
  416.3 4.8 collective-permute-done.4
  452.4 5.8 %collective-permute-done.2 = bf16[4,32,256]{2,1,0:T(8,128)(2,1)S(1)} collective-permute-done((bf16[4,32,256]{2,1,0:T(8,128)(2,1)S(1)}, bf16[4,32,256]{2,1,0:T(8,128)(2,1)S(1)}, u32[]{:S(2)}, u32[]{:S(2)}) %collective-permute-start.2) | collective-permute-done | bytes 65568 | tf_op jit(solution)/shard_map/while/body/eval_jaxpr/ppermute | solution.py:45
  458.3 5.8 %collective-permute-done.3 = bf16[4,32,256]{2,1,0:T(8,128)(2,1)S(1)} collective-permute-done((bf16[4,32,256]{2,1,0:T(8,128)(2,1)S(1)}, bf16[4,32,256]{2,1,0:T(8,128)(2,1)S(1)}, u32[]{:S(2)}, u32[]{:S(2)}) %collective-permute-start.3) | collective-permute-done | bytes 65568 | tf_op jit(solution)/shard_map/while/body/eval_jaxpr/ppermute | solution.py:45
  489.9 4.8 fusion.45
  (297 shorter events, 323.5 us)
Async XLA Ops:
  29.8 6.1 %collective-permute-start.5 = (bf16[4,32,256]{2,1,0:T(8,128)(2,1)S(1)}, bf16[4,32,256]{2,1,0:T(8,128)(2,1)S(1)}, u32[]{:S(2)}, u32[]{:S(2)}) collective-permute-start(bf16[4,32,256]{2,1,0:T(8,128)(2,1)S(1)} %broadcast_select_fusion.16), channel_id=1, source_target_pairs={{0,64},{64,0},{2,66},{66,2},{4,68},{68,4},{6,70},{70,6},{8,72},{72... | collective-permute-start | bytes 196616 | tf_op jit(solution)/shard_map/while/body/eval_jaxpr/ppermute | solution.py:45
  36.0 9.9 %collective-permute-start.6 = (bf16[4,32,256]{2,1,0:T(8,128)(2,1)S(1)}, bf16[4,32,256]{2,1,0:T(8,128)(2,1)S(1)}, u32[]{:S(2)}, u32[]{:S(2)}) collective-permute-start(bf16[4,32,256]{2,1,0:T(8,128)(2,1)S(1)} %broadcast_select_fusion.17), channel_id=1, source_target_pairs={{0,128},{128,0},{2,130},{130,2},{4,132},{132,4},{6,134},{134,6},{8... | collective-permute-start | bytes 196616 | tf_op jit(solution)/shard_map/while/body/eval_jaxpr/ppermute | solution.py:45
  41.6 6.7 %collective-permute-start.7 = (bf16[32,1024]{1,0:T(8,128)(2,1)S(1)}, bf16[32,1024]{1,0:T(8,128)(2,1)S(1)}, u32[]{:S(2)}, u32[]{:S(2)}) collective-permute-start(bf16[32,1024]{1,0:T(8,128)(2,1)S(1)} %get-tuple-element.273), channel_id=1, source_target_pairs={{2,0},{4,2},{6,4},{8,6},{10,8},{12,10},{14,12},{16,14},{18,16},{20... | collective-permute-start | bytes 196616 | tf_op jit(solution)/shard_map/while/body/eval_jaxpr/ppermute | solution.py:31
  43.6 10.8 %collective-permute-start.8 = (bf16[32,1024]{1,0:T(8,128)(2,1)S(1)}, bf16[32,1024]{1,0:T(8,128)(2,1)S(1)}, u32[]{:S(2)}, u32[]{:S(2)}) collective-permute-start(bf16[32,1024]{1,0:T(8,128)(2,1)S(1)} %get-tuple-element.273), channel_id=1, source_target_pairs={{0,2},{2,4},{4,6},{6,8},{8,10},{10,12},{12,14},{14,16},{16,18},{18... | collective-permute-start | bytes 196616 | tf_op jit(solution)/shard_map/while/body/eval_jaxpr/ppermute | solution.py:29
  87.1 8.3 %collective-permute-start.6 = (bf16[4,32,256]{2,1,0:T(8,128)(2,1)S(1)}, bf16[4,32,256]{2,1,0:T(8,128)(2,1)S(1)}, u32[]{:S(2)}, u32[]{:S(2)}) collective-permute-start(bf16[4,32,256]{2,1,0:T(8,128)(2,1)S(1)} %broadcast_select_fusion.17), channel_id=1, source_target_pairs={{0,128},{128,0},{2,130},{130,2},{4,132},{132,4},{6,134},{134,6},{8... | collective-permute-start | bytes 196616 | tf_op jit(solution)/shard_map/while/body/eval_jaxpr/ppermute | solution.py:45
  90.4 7.4 %collective-permute-start.7 = (bf16[32,1024]{1,0:T(8,128)(2,1)S(1)}, bf16[32,1024]{1,0:T(8,128)(2,1)S(1)}, u32[]{:S(2)}, u32[]{:S(2)}) collective-permute-start(bf16[32,1024]{1,0:T(8,128)(2,1)S(1)} %get-tuple-element.273), channel_id=1, source_target_pairs={{2,0},{4,2},{6,4},{8,6},{10,8},{12,10},{14,12},{16,14},{18,16},{20... | collective-permute-start | bytes 196616 | tf_op jit(solution)/shard_map/while/body/eval_jaxpr/ppermute | solution.py:31
  92.3 10.1 %collective-permute-start.8 = (bf16[32,1024]{1,0:T(8,128)(2,1)S(1)}, bf16[32,1024]{1,0:T(8,128)(2,1)S(1)}, u32[]{:S(2)}, u32[]{:S(2)}) collective-permute-start(bf16[32,1024]{1,0:T(8,128)(2,1)S(1)} %get-tuple-element.273), channel_id=1, source_target_pairs={{0,2},{2,4},{4,6},{6,8},{8,10},{10,12},{12,14},{14,16},{16,18},{18... | collective-permute-start | bytes 196616 | tf_op jit(solution)/shard_map/while/body/eval_jaxpr/ppermute | solution.py:29
  135.1 9.0 %collective-permute-start.6 = (bf16[4,32,256]{2,1,0:T(8,128)(2,1)S(1)}, bf16[4,32,256]{2,1,0:T(8,128)(2,1)S(1)}, u32[]{:S(2)}, u32[]{:S(2)}) collective-permute-start(bf16[4,32,256]{2,1,0:T(8,128)(2,1)S(1)} %broadcast_select_fusion.17), channel_id=1, source_target_pairs={{0,128},{128,0},{2,130},{130,2},{4,132},{132,4},{6,134},{134,6},{8... | collective-permute-start | bytes 196616 | tf_op jit(solution)/shard_map/while/body/eval_jaxpr/ppermute | solution.py:45
  139.0 7.4 %collective-permute-start.7 = (bf16[32,1024]{1,0:T(8,128)(2,1)S(1)}, bf16[32,1024]{1,0:T(8,128)(2,1)S(1)}, u32[]{:S(2)}, u32[]{:S(2)}) collective-permute-start(bf16[32,1024]{1,0:T(8,128)(2,1)S(1)} %get-tuple-element.273), channel_id=1, source_target_pairs={{2,0},{4,2},{6,4},{8,6},{10,8},{12,10},{14,12},{16,14},{18,16},{20... | collective-permute-start | bytes 196616 | tf_op jit(solution)/shard_map/while/body/eval_jaxpr/ppermute | solution.py:31
  140.9 10.1 %collective-permute-start.8 = (bf16[32,1024]{1,0:T(8,128)(2,1)S(1)}, bf16[32,1024]{1,0:T(8,128)(2,1)S(1)}, u32[]{:S(2)}, u32[]{:S(2)}) collective-permute-start(bf16[32,1024]{1,0:T(8,128)(2,1)S(1)} %get-tuple-element.273), channel_id=1, source_target_pairs={{0,2},{2,4},{4,6},{6,8},{8,10},{10,12},{12,14},{14,16},{16,18},{18... | collective-permute-start | bytes 196616 | tf_op jit(solution)/shard_map/while/body/eval_jaxpr/ppermute | solution.py:29
  184.0 8.3 %collective-permute-start.6 = (bf16[4,32,256]{2,1,0:T(8,128)(2,1)S(1)}, bf16[4,32,256]{2,1,0:T(8,128)(2,1)S(1)}, u32[]{:S(2)}, u32[]{:S(2)}) collective-permute-start(bf16[4,32,256]{2,1,0:T(8,128)(2,1)S(1)} %broadcast_select_fusion.17), channel_id=1, source_target_pairs={{0,128},{128,0},{2,130},{130,2},{4,132},{132,4},{6,134},{134,6},{8... | collective-permute-start | bytes 196616 | tf_op jit(solution)/shard_map/while/body/eval_jaxpr/ppermute | solution.py:45
  186.1 8.6 %collective-permute-start.7 = (bf16[32,1024]{1,0:T(8,128)(2,1)S(1)}, bf16[32,1024]{1,0:T(8,128)(2,1)S(1)}, u32[]{:S(2)}, u32[]{:S(2)}) collective-permute-start(bf16[32,1024]{1,0:T(8,128)(2,1)S(1)} %get-tuple-element.273), channel_id=1, source_target_pairs={{2,0},{4,2},{6,4},{8,6},{10,8},{12,10},{14,12},{16,14},{18,16},{20... | collective-permute-start | bytes 196616 | tf_op jit(solution)/shard_map/while/body/eval_jaxpr/ppermute | solution.py:31
  188.0 10.1 %collective-permute-start.8 = (bf16[32,1024]{1,0:T(8,128)(2,1)S(1)}, bf16[32,1024]{1,0:T(8,128)(2,1)S(1)}, u32[]{:S(2)}, u32[]{:S(2)}) collective-permute-start(bf16[32,1024]{1,0:T(8,128)(2,1)S(1)} %get-tuple-element.273), channel_id=1, source_target_pairs={{0,2},{2,4},{4,6},{6,8},{8,10},{10,12},{12,14},{14,16},{16,18},{18... | collective-permute-start | bytes 196616 | tf_op jit(solution)/shard_map/while/body/eval_jaxpr/ppermute | solution.py:29
  231.3 8.7 %collective-permute-start.6 = (bf16[4,32,256]{2,1,0:T(8,128)(2,1)S(1)}, bf16[4,32,256]{2,1,0:T(8,128)(2,1)S(1)}, u32[]{:S(2)}, u32[]{:S(2)}) collective-permute-start(bf16[4,32,256]{2,1,0:T(8,128)(2,1)S(1)} %broadcast_select_fusion.17), channel_id=1, source_target_pairs={{0,128},{128,0},{2,130},{130,2},{4,132},{132,4},{6,134},{134,6},{8... | collective-permute-start | bytes 196616 | tf_op jit(solution)/shard_map/while/body/eval_jaxpr/ppermute | solution.py:45
  235.7 6.7 %collective-permute-start.7 = (bf16[32,1024]{1,0:T(8,128)(2,1)S(1)}, bf16[32,1024]{1,0:T(8,128)(2,1)S(1)}, u32[]{:S(2)}, u32[]{:S(2)}) collective-permute-start(bf16[32,1024]{1,0:T(8,128)(2,1)S(1)} %get-tuple-element.273), channel_id=1, source_target_pairs={{2,0},{4,2},{6,4},{8,6},{10,8},{12,10},{14,12},{16,14},{18,16},{20... | collective-permute-start | bytes 196616 | tf_op jit(solution)/shard_map/while/body/eval_jaxpr/ppermute | solution.py:31
  237.6 10.1 %collective-permute-start.8 = (bf16[32,1024]{1,0:T(8,128)(2,1)S(1)}, bf16[32,1024]{1,0:T(8,128)(2,1)S(1)}, u32[]{:S(2)}, u32[]{:S(2)}) collective-permute-start(bf16[32,1024]{1,0:T(8,128)(2,1)S(1)} %get-tuple-element.273), channel_id=1, source_target_pairs={{0,2},{2,4},{4,6},{6,8},{8,10},{10,12},{12,14},{14,16},{16,18},{18... | collective-permute-start | bytes 196616 | tf_op jit(solution)/shard_map/while/body/eval_jaxpr/ppermute | solution.py:29
  281.0 8.2 %collective-permute-start.6 = (bf16[4,32,256]{2,1,0:T(8,128)(2,1)S(1)}, bf16[4,32,256]{2,1,0:T(8,128)(2,1)S(1)}, u32[]{:S(2)}, u32[]{:S(2)}) collective-permute-start(bf16[4,32,256]{2,1,0:T(8,128)(2,1)S(1)} %broadcast_select_fusion.17), channel_id=1, source_target_pairs={{0,128},{128,0},{2,130},{130,2},{4,132},{132,4},{6,134},{134,6},{8... | collective-permute-start | bytes 196616 | tf_op jit(solution)/shard_map/while/body/eval_jaxpr/ppermute | solution.py:45
  282.9 8.7 %collective-permute-start.7 = (bf16[32,1024]{1,0:T(8,128)(2,1)S(1)}, bf16[32,1024]{1,0:T(8,128)(2,1)S(1)}, u32[]{:S(2)}, u32[]{:S(2)}) collective-permute-start(bf16[32,1024]{1,0:T(8,128)(2,1)S(1)} %get-tuple-element.273), channel_id=1, source_target_pairs={{2,0},{4,2},{6,4},{8,6},{10,8},{12,10},{14,12},{16,14},{18,16},{20... | collective-permute-start | bytes 196616 | tf_op jit(solution)/shard_map/while/body/eval_jaxpr/ppermute | solution.py:31
  284.8 10.1 %collective-permute-start.8 = (bf16[32,1024]{1,0:T(8,128)(2,1)S(1)}, bf16[32,1024]{1,0:T(8,128)(2,1)S(1)}, u32[]{:S(2)}, u32[]{:S(2)}) collective-permute-start(bf16[32,1024]{1,0:T(8,128)(2,1)S(1)} %get-tuple-element.273), channel_id=1, source_target_pairs={{0,2},{2,4},{4,6},{6,8},{8,10},{10,12},{12,14},{14,16},{16,18},{18... | collective-permute-start | bytes 196616 | tf_op jit(solution)/shard_map/while/body/eval_jaxpr/ppermute | solution.py:29
  322.2 7.4 %collective-permute-start.5 = (bf16[4,32,256]{2,1,0:T(8,128)(2,1)S(1)}, bf16[4,32,256]{2,1,0:T(8,128)(2,1)S(1)}, u32[]{:S(2)}, u32[]{:S(2)}) collective-permute-start(bf16[4,32,256]{2,1,0:T(8,128)(2,1)S(1)} %broadcast_select_fusion.16), channel_id=1, source_target_pairs={{0,64},{64,0},{2,66},{66,2},{4,68},{68,4},{6,70},{70,6},{8,72},{72... | collective-permute-start | bytes 196616 | tf_op jit(solution)/shard_map/while/body/eval_jaxpr/ppermute | solution.py:45
  329.6 8.4 %collective-permute-start.6 = (bf16[4,32,256]{2,1,0:T(8,128)(2,1)S(1)}, bf16[4,32,256]{2,1,0:T(8,128)(2,1)S(1)}, u32[]{:S(2)}, u32[]{:S(2)}) collective-permute-start(bf16[4,32,256]{2,1,0:T(8,128)(2,1)S(1)} %broadcast_select_fusion.17), channel_id=1, source_target_pairs={{0,128},{128,0},{2,130},{130,2},{4,132},{132,4},{6,134},{134,6},{8... | collective-permute-start | bytes 196616 | tf_op jit(solution)/shard_map/while/body/eval_jaxpr/ppermute | solution.py:45
  332.4 8.0 %collective-permute-start.7 = (bf16[32,1024]{1,0:T(8,128)(2,1)S(1)}, bf16[32,1024]{1,0:T(8,128)(2,1)S(1)}, u32[]{:S(2)}, u32[]{:S(2)}) collective-permute-start(bf16[32,1024]{1,0:T(8,128)(2,1)S(1)} %get-tuple-element.273), channel_id=1, source_target_pairs={{2,0},{4,2},{6,4},{8,6},{10,8},{12,10},{14,12},{16,14},{18,16},{20... | collective-permute-start | bytes 196616 | tf_op jit(solution)/shard_map/while/body/eval_jaxpr/ppermute | solution.py:31
  334.3 10.1 %collective-permute-start.8 = (bf16[32,1024]{1,0:T(8,128)(2,1)S(1)}, bf16[32,1024]{1,0:T(8,128)(2,1)S(1)}, u32[]{:S(2)}, u32[]{:S(2)}) collective-permute-start(bf16[32,1024]{1,0:T(8,128)(2,1)S(1)} %get-tuple-element.273), channel_id=1, source_target_pairs={{0,2},{2,4},{4,6},{6,8},{8,10},{10,12},{12,14},{14,16},{16,18},{18... | collective-permute-start | bytes 196616 | tf_op jit(solution)/shard_map/while/body/eval_jaxpr/ppermute | solution.py:29
  377.6 8.2 %collective-permute-start.6 = (bf16[4,32,256]{2,1,0:T(8,128)(2,1)S(1)}, bf16[4,32,256]{2,1,0:T(8,128)(2,1)S(1)}, u32[]{:S(2)}, u32[]{:S(2)}) collective-permute-start(bf16[4,32,256]{2,1,0:T(8,128)(2,1)S(1)} %broadcast_select_fusion.17), channel_id=1, source_target_pairs={{0,128},{128,0},{2,130},{130,2},{4,132},{132,4},{6,134},{134,6},{8... | collective-permute-start | bytes 196616 | tf_op jit(solution)/shard_map/while/body/eval_jaxpr/ppermute | solution.py:45
  381.3 6.8 %collective-permute-start.7 = (bf16[32,1024]{1,0:T(8,128)(2,1)S(1)}, bf16[32,1024]{1,0:T(8,128)(2,1)S(1)}, u32[]{:S(2)}, u32[]{:S(2)}) collective-permute-start(bf16[32,1024]{1,0:T(8,128)(2,1)S(1)} %get-tuple-element.273), channel_id=1, source_target_pairs={{2,0},{4,2},{6,4},{8,6},{10,8},{12,10},{14,12},{16,14},{18,16},{20... | collective-permute-start | bytes 196616 | tf_op jit(solution)/shard_map/while/body/eval_jaxpr/ppermute | solution.py:31
  383.2 10.1 %collective-permute-start.8 = (bf16[32,1024]{1,0:T(8,128)(2,1)S(1)}, bf16[32,1024]{1,0:T(8,128)(2,1)S(1)}, u32[]{:S(2)}, u32[]{:S(2)}) collective-permute-start(bf16[32,1024]{1,0:T(8,128)(2,1)S(1)} %get-tuple-element.273), channel_id=1, source_target_pairs={{0,2},{2,4},{4,6},{6,8},{8,10},{10,12},{12,14},{14,16},{16,18},{18... | collective-permute-start | bytes 196616 | tf_op jit(solution)/shard_map/while/body/eval_jaxpr/ppermute | solution.py:29
  426.6 8.4 %collective-permute-start.6 = (bf16[4,32,256]{2,1,0:T(8,128)(2,1)S(1)}, bf16[4,32,256]{2,1,0:T(8,128)(2,1)S(1)}, u32[]{:S(2)}, u32[]{:S(2)}) collective-permute-start(bf16[4,32,256]{2,1,0:T(8,128)(2,1)S(1)} %broadcast_select_fusion.17), channel_id=1, source_target_pairs={{0,128},{128,0},{2,130},{130,2},{4,132},{132,4},{6,134},{134,6},{8... | collective-permute-start | bytes 196616 | tf_op jit(solution)/shard_map/while/body/eval_jaxpr/ppermute | solution.py:45
  429.3 8.0 %collective-permute-start.7 = (bf16[32,1024]{1,0:T(8,128)(2,1)S(1)}, bf16[32,1024]{1,0:T(8,128)(2,1)S(1)}, u32[]{:S(2)}, u32[]{:S(2)}) collective-permute-start(bf16[32,1024]{1,0:T(8,128)(2,1)S(1)} %get-tuple-element.273), channel_id=1, source_target_pairs={{2,0},{4,2},{6,4},{8,6},{10,8},{12,10},{14,12},{16,14},{18,16},{20... | collective-permute-start | bytes 196616 | tf_op jit(solution)/shard_map/while/body/eval_jaxpr/ppermute | solution.py:31
  431.2 10.1 %collective-permute-start.8 = (bf16[32,1024]{1,0:T(8,128)(2,1)S(1)}, bf16[32,1024]{1,0:T(8,128)(2,1)S(1)}, u32[]{:S(2)}, u32[]{:S(2)}) collective-permute-start(bf16[32,1024]{1,0:T(8,128)(2,1)S(1)} %get-tuple-element.273), channel_id=1, source_target_pairs={{0,2},{2,4},{4,6},{6,8},{8,10},{10,12},{12,14},{14,16},{16,18},{18... | collective-permute-start | bytes 196616 | tf_op jit(solution)/shard_map/while/body/eval_jaxpr/ppermute | solution.py:29
  474.7 8.4 %collective-permute-start.6 = (bf16[4,32,256]{2,1,0:T(8,128)(2,1)S(1)}, bf16[4,32,256]{2,1,0:T(8,128)(2,1)S(1)}, u32[]{:S(2)}, u32[]{:S(2)}) collective-permute-start(bf16[4,32,256]{2,1,0:T(8,128)(2,1)S(1)} %broadcast_select_fusion.17), channel_id=1, source_target_pairs={{0,128},{128,0},{2,130},{130,2},{4,132},{132,4},{6,134},{134,6},{8... | collective-permute-start | bytes 196616 | tf_op jit(solution)/shard_map/while/body/eval_jaxpr/ppermute | solution.py:45
  477.9 7.5 %collective-permute-start.7 = (bf16[32,1024]{1,0:T(8,128)(2,1)S(1)}, bf16[32,1024]{1,0:T(8,128)(2,1)S(1)}, u32[]{:S(2)}, u32[]{:S(2)}) collective-permute-start(bf16[32,1024]{1,0:T(8,128)(2,1)S(1)} %get-tuple-element.273), channel_id=1, source_target_pairs={{2,0},{4,2},{6,4},{8,6},{10,8},{12,10},{14,12},{16,14},{18,16},{20... | collective-permute-start | bytes 196616 | tf_op jit(solution)/shard_map/while/body/eval_jaxpr/ppermute | solution.py:31
  479.8 10.1 %collective-permute-start.8 = (bf16[32,1024]{1,0:T(8,128)(2,1)S(1)}, bf16[32,1024]{1,0:T(8,128)(2,1)S(1)}, u32[]{:S(2)}, u32[]{:S(2)}) collective-permute-start(bf16[32,1024]{1,0:T(8,128)(2,1)S(1)} %get-tuple-element.273), channel_id=1, source_target_pairs={{0,2},{2,4},{4,6},{6,8},{8,10},{10,12},{12,14},{14,16},{16,18},{18... | collective-permute-start | bytes 196616 | tf_op jit(solution)/shard_map/while/body/eval_jaxpr/ppermute | solution.py:29
  (66 other events, 301.7 us)
where the time goes:
time: 496 us; the launch traced here: 495 us
  waiting for transfers between devices  289 us (58%)
  starting transfers between devices  117 us (24%)
  matrix products  75.3 us (15%)
  other arithmetic  11.5 us (2%)
    ppermute x70, waiting for transfers between devices, swapped(): return lax.ppermute(block, axis, route)  244 us
    ppermute x70, starting transfers between devices, swapped(): return lax.ppermute(block, axis, route)  73.7 us
    dot_general x10, matrix products, contract_last(): lax.dot_general(left, right, (((1,), (1,)), ((), ())), preferred_element_...  47.8 us
    ppermute x10, waiting for transfers between devices, padded_2(): lax.ppermute(tail, axis, [(i, (i + 1) % count) for i in range(ends)])  45.2 us
    ppermute x10, starting transfers between devices, padded_2(): lax.ppermute(tail, axis, [(i, (i + 1) % count) for i in range(ends)])  24 us
    dot_general x10, matrix products, advance(): jnp.einsum('mrk,mvk->rv', received, tract_in, preferred_element_type=jnp....  22.9 us
    ppermute x10, starting transfers between devices, padded_2(): lax.ppermute(head, axis, [((i + 1) % count, i) for i in range(ends)])  19.2 us
  transfers between devices with their start and end apart: 90, of which 78 were waited for; matrix products, arithmetic and copies ran while one was open for 5% of the time, Pallas kernels for 0%

commit v1 on v0

v1 whole, which is shorter than its diff:
```python
import functools
import math

import jax
import jax.numpy as jnp
from jax import lax
from jax.experimental import pallas as pl
from jax.experimental.pallas import tpu as pltpu
from jax.sharding import PartitionSpec as P


TILE_V = 1024
HW = 1024
BLOCK = 256
MATCH = 4
BASIS = (1, 2, 6, 8, 16, 48, 112)

time_step = 0.1
noise_gain = 0.5
shift_a = 0.7
damp_b = 0.8
drive_level = 0.5
band_gain = 1.0
tract_gain = 0.5

VMEM = pl.BlockSpec(memory_space=pltpu.VMEM)
PARAMS = pltpu.CompilerParams(vmem_limit_bytes=10 << 20)


def basis_rows(basis, bits):
    rows = [[basis[j] >> i & 1 for j in range(bits)] + [int(i == j) for j in range(bits)] for i in range(bits)]
    for col in range(bits):
        pivot = next(r for r in range(col, bits) if rows[r][col])
        rows[col], rows[pivot] = rows[pivot], rows[col]
        for r in range(bits):
            if r != col and rows[r][col]:
                rows[r] = [a ^ b for a, b in zip(rows[r], rows[col])]
    return [[i for i in range(bits) if rows[j][bits + i]] for j in range(bits)]


def nt(left, right):
    return lax.dot_general(left, right, (((1,), (1,)), ((), ())), preferred_element_type=jnp.float32)


def project(vb, tract_out_ref, packed_ref):
    for m in range(MATCH):
        packed_ref[m] = jnp.dot(vb, tract_out_ref[m], preferred_element_type=jnp.float32).astype(jnp.bfloat16)


def first_kernel(v_ref, tract_out_ref, packed_ref):
    vb = v_ref[...].astype(jnp.bfloat16)
    project(vb, tract_out_ref, packed_ref)
    for j in range(HW // BLOCK):
        packed_ref[MATCH + j] = vb[:, j * BLOCK : (j + 1) * BLOCK]


def center_kernel(packed_ref, weight_ref, out_ref):
    vb = jnp.concatenate([packed_ref[MATCH + j] for j in range(TILE_V // BLOCK)], axis=1)
    for i in range(TILE_V // BLOCK):
        rows = slice(i * BLOCK, (i + 1) * BLOCK)
        out_ref[:, rows] = nt(vb, weight_ref[rows, HW : HW + TILE_V])


def sides_kernel(
    n, odd_ref, near_ref, far_ref, center_ref, weight_ref, v_ref, w_ref, scale_ref, kick_ref, base_ref, w_out
):
    odd = odd_ref[...] > 0.5
    left, right = [], []
    for j in range(HW // BLOCK):
        near, far = near_ref[MATCH + j].astype(jnp.float32), far_ref[j].astype(jnp.float32)
        left.append(jnp.where(odd, near, far).astype(jnp.bfloat16))
        right.append(jnp.where(odd, far, near).astype(jnp.bfloat16))
    row = lax.broadcasted_iota(jnp.int32, (BLOCK, BLOCK), 0)
    col = lax.broadcasted_iota(jnp.int32, (BLOCK, BLOCK), 1)

    def weights(i, column, keep=None):
        block = weight_ref[i * BLOCK : (i + 1) * BLOCK, column : column + BLOCK]
        if keep is None:
            return block
        return jnp.where(keep, block.astype(jnp.float32), 0.0).astype(jnp.bfloat16)

    for i in range(TILE_V // BLOCK):
        cols = slice(i * BLOCK, (i + 1) * BLOCK)
        band = center_ref[:, cols]
        for j in range(i, HW // BLOCK):
            band += nt(left[j], weights(i, j * BLOCK, col >= row if j == i else None))
        for j in range(i + 1):
            band += nt(right[j], weights(i, HW + TILE_V + j * BLOCK, col <= row if j == i else None))
        v, w = v_ref[:, cols], w_ref[:, cols]
        rate = v - v * v * v / 3.0 - w + band_gain * band + drive_level
        base_ref[:, cols] = v + time_step * rate + noise_gain * math.sqrt(time_step) * kick_ref[n, :, cols]
        w_out[:, cols] = w + time_step * scale_ref[:, cols] * (v + shift_a - damp_b * w)


def update_kernel(received_ref, tract_in_ref, base_ref, tract_out_ref, v_out, packed_ref):
    received = jnp.concatenate([received_ref[m] for m in range(MATCH)], axis=1)
    rounded = []
    for i in range(TILE_V // BLOCK):
        cols = slice(i * BLOCK, (i + 1) * BLOCK)
        tract = jnp.dot(received, tract_in_ref[:, cols], preferred_element_type=jnp.float32)
        v_new = base_ref[:, cols] + time_step * tract_gain * tract
        v_out[:, cols] = v_new
        rounded.append(v_new.astype(jnp.bfloat16))
        packed_ref[MATCH + i] = rounded[i]
    project(jnp.concatenate(rounded, axis=1), tract_out_ref, packed_ref)


def per_device(
    voltage, recovery, increments, band_weight, time_scale, tract_in, tract_out, matching_masks, tract_on
):
    count = lax.axis_size("tile")
    bits = count.bit_length() - 1
    rows = voltage.shape[0]
    rank = tract_out.shape[2]
    parities = basis_rows(BASIS, bits)
    odd = jnp.full((rows, BLOCK), jnp.bitwise_and(lax.axis_index("tile"), 1), jnp.float32)
    far_route = [(i, i + 1) for i in range(1, count - 1, 2)] + [(i + 1, i) for i in range(1, count - 1, 2)]

    def pick(j, arrived, kept):
        folded = sum(jnp.right_shift(matching_masks, b) for b in parities[j])
        chosen = jnp.bitwise_and(folded, 1) == 1
        return jnp.where(chosen[:, None, None], arrived, kept)

    def swap(block, mask):
        return lax.ppermute(block, "tile", [(i, i ^ mask) for i in range(count)])

    state = jax.ShapeDtypeStruct(voltage.shape, jnp.float32)
    packed = jax.ShapeDtypeStruct((MATCH + HW // BLOCK, rows, BLOCK), jnp.bfloat16)
    weight_flops = 2 * rows * TILE_V * TILE_V

    def cost(blocks, nbytes):
        return pl.CostEstimate(flops=int(blocks * weight_flops), bytes_accessed=nbytes, transcendentals=0)

    first = pl.pallas_call(
        first_kernel, out_shape=packed, in_specs=[VMEM] * 2, out_specs=VMEM, name="first", compiler_params=PARAMS
    )
    center = pl.pallas_call(
        center_kernel, out_shape=state, in_specs=[VMEM] * 2, out_specs=VMEM, name="center",
        compiler_params=PARAMS, cost_estimate=cost(1, 2 << 20),
    )

    def sides(n, *operands):
        return pl.pallas_call(
            functools.partial(sides_kernel, n), out_shape=(state, state), in_specs=[VMEM] * 9, out_specs=(VMEM,) * 2,
            name="sides", input_output_aliases={6: 1}, compiler_params=PARAMS, cost_estimate=cost(1.25, 3 << 20),
        )(*operands)

    update = pl.pallas_call(
        update_kernel, out_shape=(state, packed), in_specs=[VMEM] * 4, out_specs=(VMEM,) * 2,
        name="update", input_output_aliases={2: 0}, compiler_params=PARAMS, cost_estimate=cost(2, 5 << 20),
    )
    scale_row = time_scale[None, :]
    inward_rows = tract_in.transpose(0, 2, 1).reshape(MATCH * rank, TILE_V)

    def advance(n, carry, kicks):
        v, w, both = carry
        inward, outward, weight = [
            pltpu.with_memory_space_constraint(a, pltpu.VMEM) for a in (inward_rows, tract_out, band_weight)
        ]
        own = both[MATCH:]
        far = lax.ppermute(own, "tile", far_route)
        middle = center(both, weight)
        near = swap(both, BASIS[0])
        moving, arrived = both[:MATCH], near[:MATCH]
        for j, mask in enumerate(BASIS[1:]):
            moving = pick(j, arrived, moving)
            arrived = swap(moving, mask)
        base, w = sides(n, odd, near, far, middle, weight, v, w, scale_row, kicks)
        received = pick(len(BASIS) - 1, arrived, moving) * tract_on[0].astype(jnp.bfloat16)[:, None, None]
        v, both = update(received, inward, base, outward)
        return v, w, both

    steps = increments.shape[0]
    unrolled = next(n for n in (5, 2, 1) if steps % n == 0)

    def several(carry, kicks):
        for n in range(unrolled):
            carry = advance(n, carry, kicks)
        return carry, None

    both = first(voltage, tract_out)
    (voltage_end, recovery_end, _), _ = lax.scan(
        several, (voltage, recovery, both), increments.reshape(steps // unrolled, unrolled, rows, TILE_V)
    )
    return voltage_end, recovery_end


def solution(mesh):
    placed = (
        P("real", "tile"),
        P("real", "tile"),
        P(None, "real", "tile"),
        P("tile", None),
        P("tile"),
        P(None, "tile", None),
        P(None, "tile", None),
        P(),
        P("tile", None),
    )
    return jax.shard_map(
        per_device,
        mesh=mesh,
        in_specs=placed,
        out_specs=(P("real", "tile"), P("real", "tile")),
        check_vma=False,
    )
```

time: 496 us -> 383 us (0.77)
  waiting for transfers between devices: 289 us -> 198 us
  matrix products: 75.3 us -> 0 us
  Pallas kernels: 0 us -> 26.4 us
  local copies, waits for them, and re-layouts: 0.82 us -> 24.5 us
    ppermute x90 -> x80, waiting for transfers between devices: 289 us -> 198 us  [the longest x70 175 us: swap(): return lax.ppermute(block, 'tile', [(i, i ^ mask) for i in range(count)])]
    dot_general x30 -> x0, matrix products: 75.3 us -> none  [the longest x10 47.8 us: contract_last(): lax.dot_general(left, right, (((1,), (1,)), ((), ())), preferred_element_...]
    pallas_call x0 -> x31, Pallas kernels: none -> 26.4 us  [the longest x10 9.01 us: sides(): pl.pallas_call(functools.partial(sides_kernel, n), out_shape=(state, stat...]
    while x10 -> x20, local copies, waits for them, and re-layouts: 0.11 us -> 16.4 us
    select_n x61 -> x50, other arithmetic: 11 us -> 5.16 us  [pick(): return jnp.where(chosen[:, None, None], arrived, kept)]
    ppermute x90 -> x80, starting transfers between devices: 117 us -> 118 us  [the longest x70 91.4 us: swap(): return lax.ppermute(block, 'tile', [(i, i ^ mask) for i in range(count)])]
  transfers between devices with their start and end apart: 90 -> 80, of which waited for: 78 -> 70; matrix products, arithmetic and copies ran while one was open for 5% -> 1% of each run, Pallas kernels for 0% -> 4%
where the time goes in v1:
time: 383 us; the launch traced here: 378 us
  waiting for transfers between devices  198 us (52%)
  starting transfers between devices  118 us (31%)
  Pallas kernels  26.4 us (7%)
  local copies, waits for them, and re-layouts  24.5 us (6%)
  other arithmetic  9.17 us (2%)
    ppermute x70, waiting for transfers between devices, swap(): return lax.ppermute(block, 'tile', [(i, i ^ mask) for i in range(count)])  175 us
    ppermute x70, starting transfers between devices, swap(): return lax.ppermute(block, 'tile', [(i, i ^ mask) for i in range(count)])  91.4 us
    ppermute x10, starting transfers between devices, advance(): far = lax.ppermute(own, 'tile', far_route)  26.7 us
    ppermute x10, waiting for transfers between devices, advance(): far = lax.ppermute(own, 'tile', far_route)  22.8 us
    while x20, local copies, waits for them, and re-layouts  16.4 us
    pallas_call x10, Pallas kernels, sides(): pl.pallas_call(functools.partial(sides_kernel, n), out_shape=(state, stat...  9.01 us
    pallas_call x10, Pallas kernels, advance(): v, both = update(received, inward, base, outward)  8.22 us
  transfers between devices with their start and end apart: 80, of which 70 were waited for; matrix products, arithmetic and copies ran while one was open for 1% of the time, Pallas kernels for 4%

profile of v1, /device:TPU:32, one launch (start us, length us, event | category | flops | bytes accessed | tf_op | source)
XLA Modules:
  0.0 377.6 jit_solution(10172978354755512023)
XLA Ops:
  4.3 4.2 %copy.21 = bf16[4,256,1024]{2,1,0:T(8,128)(2,1)} copy(bf16[4,256,1024]{1,2,0:T(8,128)(2,1)} %bitcast.16) | data formatting | bytes 4194304 | tf_op jit(solution)/shard_map/transpose | solution.py:153
  8.5 368.4 %while.17 = (s32[]{:T(128)}, f32[32,1024]{1,0:T(8,128)S(1)}, f32[32,1024]{1,0:T(8,128)S(1)}, bf16[8,32,256]{2,1,0:T(8,128)(2,1)S(1)}, s32[4]{0:T(128)S(1)}, /*in...) while((s32[]{:T(128)}, f32[32,1024]{1,0:T(8,128)S(1)}, ...), condition=%wide.region_1.2_spmd.clone, body=%wide.region_0.1_spmd.clone.sunk | while | flops 1427374208 | bytes 165382224 | solution.py:182
  32.9 4.0 %collective-permute-start.7 = (bf16[4,32,256]{2,1,0:T(8,128)(2,1)S(1)}, bf16[4,32,256]{2,1,0:T(8,128)(2,1)S(1)}, u32[]{:S(2)}, u32[]{:S(2)}) collective-permute-start(bf16[4,32,256]{2,1,0:T(8,128)(2,1)S(1)} %get-tuple-element.364), channel_id=1, source_target_pairs={{2,4},{6,8},{10,12},{14,16},{18,20},{22,24},{26,28},{30,32},{34,36... | collective-permute-start | bytes 196616 | tf_op jit(solution)/shard_map/while/body/eval_jaxpr/ppermute | solution.py:161
  37.0 4.2 %collective-permute-start.6 = (bf16[4,32,256]{2,1,0:T(8,128)(2,1)S(1)}, bf16[4,32,256]{2,1,0:T(8,128)(2,1)S(1)}, u32[]{:S(2)}, u32[]{:S(2)}) collective-permute-start(bf16[4,32,256]{2,1,0:T(8,128)(2,1)S(1)} %broadcast_select_fusion.54), channel_id=1, source_target_pairs={{0,224},{2,226},{4,228},{6,230},{8,232},{10,234},{12,236},{14,238}... | collective-permute-start | bytes 196616 | tf_op jit(solution)/shard_map/while/body/eval_jaxpr/ppermute | solution.py:125
  52.2 3.9 %collective-permute-done.9 = bf16[4,32,256]{2,1,0:T(8,128)(2,1)S(1)} collective-permute-done((bf16[4,32,256]{2,1,0:T(8,128)(2,1)S(1)}, bf16[4,32,256]{2,1,0:T(8,128)(2,1)S(1)}, u32[]{:S(2)}, u32[]{:S(2)}) %collective-permute-start.9) | collective-permute-done | bytes 65568 | tf_op jit(solution)/shard_map/while/body/eval_jaxpr/ppermute | solution.py:125
  56.2 3.9 %collective-permute-start.10 = (bf16[4,32,256]{2,1,0:T(8,128)(2,1)S(1)}, bf16[4,32,256]{2,1,0:T(8,128)(2,1)S(1)}, u32[]{:S(2)}, u32[]{:S(2)}) collective-permute-start(bf16[4,32,256]{2,1,0:T(8,128)(2,1)S(1)} %broadcast_select_fusion.55), channel_id=1, source_target_pairs={{0,12},{2,14},{4,8},{6,10},{8,4},{10,6},{12,0},{14,2},{16,28},{18,... | collective-permute-start | bytes 196616 | tf_op jit(solution)/shard_map/while/body/eval_jaxpr/ppermute | solution.py:125
  69.0 4.3 %collective-permute-done.12 = bf16[4,32,256]{2,1,0:T(8,128)(2,1)S(1)} collective-permute-done((bf16[4,32,256]{2,1,0:T(8,128)(2,1)S(1)}, bf16[4,32,256]{2,1,0:T(8,128)(2,1)S(1)}, u32[]{:S(2)}, u32[]{:S(2)}) %collective-permute-start.12) | collective-permute-done | bytes 65568 | tf_op jit(solution)/shard_map/while/body/eval_jaxpr/ppermute | solution.py:125
  79.2 5.3 %collective-permute-done.15.far_ref = bf16[4,32,256]{2,1,0:T(8,128)(2,1)S(1)} collective-permute-done((bf16[4,32,256]{2,1,0:T(8,128)(2,1)S(1)}, bf16[4,32,256]{2,1,0:T(8,128)(2,1)S(1)}, u32[]{:S(2)}, u32[]{:S(2)}) %collective-permute-start.15) | collective-permute-done | bytes 65568 | tf_op jit(solution)/shard_map/while/body/eval_jaxpr/ppermute | solution.py:161
  88.2 4.3 %collective-permute-done.17 = bf16[4,32,256]{2,1,0:T(8,128)(2,1)S(1)} collective-permute-done((bf16[4,32,256]{2,1,0:T(8,128)(2,1)S(1)}, bf16[4,32,256]{2,1,0:T(8,128)(2,1)S(1)}, u32[]{:S(2)}, u32[]{:S(2)}) %collective-permute-start.17) | collective-permute-done | bytes 65568 | tf_op jit(solution)/shard_map/while/body/eval_jaxpr/ppermute | solution.py:125
  99.6 4.3 %collective-permute-done.19 = bf16[4,32,256]{2,1,0:T(8,128)(2,1)S(1)} collective-permute-done((bf16[4,32,256]{2,1,0:T(8,128)(2,1)S(1)}, bf16[4,32,256]{2,1,0:T(8,128)(2,1)S(1)}, u32[]{:S(2)}, u32[]{:S(2)}) %collective-permute-start.19) | collective-permute-done | bytes 65568 | tf_op jit(solution)/shard_map/while/body/eval_jaxpr/ppermute | solution.py:125
  104.8 4.1 %collective-permute-done.20 = bf16[4,32,256]{2,1,0:T(8,128)(2,1)S(1)} collective-permute-done((bf16[4,32,256]{2,1,0:T(8,128)(2,1)S(1)}, bf16[4,32,256]{2,1,0:T(8,128)(2,1)S(1)}, u32[]{:S(2)}, u32[]{:S(2)}) %collective-permute-start.20) | collective-permute-done | bytes 65568 | tf_op jit(solution)/shard_map/while/body/eval_jaxpr/ppermute | solution.py:125
  114.8 5.3 %collective-permute-done.23.far_ref = bf16[4,32,256]{2,1,0:T(8,128)(2,1)S(1)} collective-permute-done((bf16[4,32,256]{2,1,0:T(8,128)(2,1)S(1)}, bf16[4,32,256]{2,1,0:T(8,128)(2,1)S(1)}, u32[]{:S(2)}, u32[]{:S(2)}) %collective-permute-start.23) | collective-permute-done | bytes 65568 | tf_op jit(solution)/shard_map/while/body/eval_jaxpr/ppermute | solution.py:161
  123.8 4.3 %collective-permute-done.25 = bf16[4,32,256]{2,1,0:T(8,128)(2,1)S(1)} collective-permute-done((bf16[4,32,256]{2,1,0:T(8,128)(2,1)S(1)}, bf16[4,32,256]{2,1,0:T(8,128)(2,1)S(1)}, u32[]{:S(2)}, u32[]{:S(2)}) %collective-permute-start.25) | collective-permute-done | bytes 65568 | tf_op jit(solution)/shard_map/while/body/eval_jaxpr/ppermute | solution.py:125
  135.1 4.4 %collective-permute-done.27 = bf16[4,32,256]{2,1,0:T(8,128)(2,1)S(1)} collective-permute-done((bf16[4,32,256]{2,1,0:T(8,128)(2,1)S(1)}, bf16[4,32,256]{2,1,0:T(8,128)(2,1)S(1)}, u32[]{:S(2)}, u32[]{:S(2)}) %collective-permute-start.27) | collective-permute-done | bytes 65568 | tf_op jit(solution)/shard_map/while/body/eval_jaxpr/ppermute | solution.py:125
  139.8 4.5 %collective-permute-done.28 = bf16[4,32,256]{2,1,0:T(8,128)(2,1)S(1)} collective-permute-done((bf16[4,32,256]{2,1,0:T(8,128)(2,1)S(1)}, bf16[4,32,256]{2,1,0:T(8,128)(2,1)S(1)}, u32[]{:S(2)}, u32[]{:S(2)}) %collective-permute-start.28) | collective-permute-done | bytes 65568 | tf_op jit(solution)/shard_map/while/body/eval_jaxpr/ppermute | solution.py:125
  150.3 4.9 %collective-permute-done.31.far_ref = bf16[4,32,256]{2,1,0:T(8,128)(2,1)S(1)} collective-permute-done((bf16[4,32,256]{2,1,0:T(8,128)(2,1)S(1)}, bf16[4,32,256]{2,1,0:T(8,128)(2,1)S(1)}, u32[]{:S(2)}, u32[]{:S(2)}) %collective-permute-start.31) | collective-permute-done | bytes 65568 | tf_op jit(solution)/shard_map/while/body/eval_jaxpr/ppermute | solution.py:161
  159.3 4.3 %collective-permute-done.33 = bf16[4,32,256]{2,1,0:T(8,128)(2,1)S(1)} collective-permute-done((bf16[4,32,256]{2,1,0:T(8,128)(2,1)S(1)}, bf16[4,32,256]{2,1,0:T(8,128)(2,1)S(1)}, u32[]{:S(2)}, u32[]{:S(2)}) %collective-permute-start.33) | collective-permute-done | bytes 65568 | tf_op jit(solution)/shard_map/while/body/eval_jaxpr/ppermute | solution.py:125
  170.6 4.4 %collective-permute-done.35 = bf16[4,32,256]{2,1,0:T(8,128)(2,1)S(1)} collective-permute-done((bf16[4,32,256]{2,1,0:T(8,128)(2,1)S(1)}, bf16[4,32,256]{2,1,0:T(8,128)(2,1)S(1)}, u32[]{:S(2)}, u32[]{:S(2)}) %collective-permute-start.35) | collective-permute-done | bytes 65568 | tf_op jit(solution)/shard_map/while/body/eval_jaxpr/ppermute | solution.py:125
  175.2 4.3 %collective-permute-done.36 = bf16[4,32,256]{2,1,0:T(8,128)(2,1)S(1)} collective-permute-done((bf16[4,32,256]{2,1,0:T(8,128)(2,1)S(1)}, bf16[4,32,256]{2,1,0:T(8,128)(2,1)S(1)}, u32[]{:S(2)}, u32[]{:S(2)}) %collective-permute-start.36) | collective-permute-done | bytes 65568 | tf_op jit(solution)/shard_map/while/body/eval_jaxpr/ppermute | solution.py:125
  196.1 4.3 %collective-permute-done.1 = bf16[4,32,256]{2,1,0:T(8,128)(2,1)S(1)} collective-permute-done((bf16[4,32,256]{2,1,0:T(8,128)(2,1)S(1)}, bf16[4,32,256]{2,1,0:T(8,128)(2,1)S(1)}, u32[]{:S(2)}, u32[]{:S(2)}) %collective-permute-start.1) | collective-permute-done | bytes 65568 | tf_op jit(solution)/shard_map/while/body/eval_jaxpr/ppermute | solution.py:125
  201.9 4.0 %collective-permute-done.2 = bf16[4,32,256]{2,1,0:T(8,128)(2,1)S(1)} collective-permute-done((bf16[4,32,256]{2,1,0:T(8,128)(2,1)S(1)}, bf16[4,32,256]{2,1,0:T(8,128)(2,1)S(1)}, u32[]{:S(2)}, u32[]{:S(2)}) %collective-permute-start.2) | collective-permute-done | bytes 65568 | tf_op jit(solution)/shard_map/while/body/eval_jaxpr/ppermute | solution.py:125
  207.8 4.1 %collective-permute-done.3 = bf16[4,32,256]{2,1,0:T(8,128)(2,1)S(1)} collective-permute-done((bf16[4,32,256]{2,1,0:T(8,128)(2,1)S(1)}, bf16[4,32,256]{2,1,0:T(8,128)(2,1)S(1)}, u32[]{:S(2)}, u32[]{:S(2)}) %collective-permute-start.3) | collective-permute-done | bytes 65568 | tf_op jit(solution)/shard_map/while/body/eval_jaxpr/ppermute | solution.py:125
  212.0 4.8 %collective-permute-done.4 = bf16[4,32,256]{2,1,0:T(8,128)(2,1)S(1)} collective-permute-done((bf16[4,32,256]{2,1,0:T(8,128)(2,1)S(1)}, bf16[4,32,256]{2,1,0:T(8,128)(2,1)S(1)}, u32[]{:S(2)}, u32[]{:S(2)}) %collective-permute-start.4) | collective-permute-done | bytes 65568 | tf_op jit(solution)/shard_map/while/body/eval_jaxpr/ppermute | solution.py:125
  233.3 4.3 %collective-permute-done.9 = bf16[4,32,256]{2,1,0:T(8,128)(2,1)S(1)} collective-permute-done((bf16[4,32,256]{2,1,0:T(8,128)(2,1)S(1)}, bf16[4,32,256]{2,1,0:T(8,128)(2,1)S(1)}, u32[]{:S(2)}, u32[]{:S(2)}) %collective-permute-start.9) | collective-permute-done | bytes 65568 | tf_op jit(solution)/shard_map/while/body/eval_jaxpr/ppermute | solution.py:125
  258.5 4.9 %collective-permute-start.14 = (bf16[4,32,256]{2,1,0:T(8,128)(2,1)S(1)}, bf16[4,32,256]{2,1,0:T(8,128)(2,1)S(1)}, u32[]{:S(2)}, u32[]{:S(2)}) collective-permute-start(bf16[4,32,256]{2,1,0:T(8,128)(2,1)S(1)} %broadcast_select_fusion.59), channel_id=1, source_target_pairs={{0,224},{2,226},{4,228},{6,230},{8,232},{10,234},{12,236},{14,238}... | collective-permute-start | bytes 196616 | tf_op jit(solution)/shard_map/while/body/eval_jaxpr/ppermute | solution.py:125
  268.9 4.3 %collective-permute-done.17 = bf16[4,32,256]{2,1,0:T(8,128)(2,1)S(1)} collective-permute-done((bf16[4,32,256]{2,1,0:T(8,128)(2,1)S(1)}, bf16[4,32,256]{2,1,0:T(8,128)(2,1)S(1)}, u32[]{:S(2)}, u32[]{:S(2)}) %collective-permute-start.17) | collective-permute-done | bytes 65568 | tf_op jit(solution)/shard_map/while/body/eval_jaxpr/ppermute | solution.py:125
  293.9 4.1 %collective-permute-start.22 = (bf16[4,32,256]{2,1,0:T(8,128)(2,1)S(1)}, bf16[4,32,256]{2,1,0:T(8,128)(2,1)S(1)}, u32[]{:S(2)}, u32[]{:S(2)}) collective-permute-start(bf16[4,32,256]{2,1,0:T(8,128)(2,1)S(1)} %broadcast_select_fusion.64), channel_id=1, source_target_pairs={{0,224},{2,226},{4,228},{6,230},{8,232},{10,234},{12,236},{14,238}... | collective-permute-start | bytes 196616 | tf_op jit(solution)/shard_map/while/body/eval_jaxpr/ppermute | solution.py:125
  304.8 4.3 %collective-permute-done.25 = bf16[4,32,256]{2,1,0:T(8,128)(2,1)S(1)} collective-permute-done((bf16[4,32,256]{2,1,0:T(8,128)(2,1)S(1)}, bf16[4,32,256]{2,1,0:T(8,128)(2,1)S(1)}, u32[]{:S(2)}, u32[]{:S(2)}) %collective-permute-start.25) | collective-permute-done | bytes 65568 | tf_op jit(solution)/shard_map/while/body/eval_jaxpr/ppermute | solution.py:125
  321.2 4.1 %collective-permute-done.28 = bf16[4,32,256]{2,1,0:T(8,128)(2,1)S(1)} collective-permute-done((bf16[4,32,256]{2,1,0:T(8,128)(2,1)S(1)}, bf16[4,32,256]{2,1,0:T(8,128)(2,1)S(1)}, u32[]{:S(2)}, u32[]{:S(2)}) %collective-permute-start.28) | collective-permute-done | bytes 65568 | tf_op jit(solution)/shard_map/while/body/eval_jaxpr/ppermute | solution.py:125
  340.4 4.3 %collective-permute-done.33 = bf16[4,32,256]{2,1,0:T(8,128)(2,1)S(1)} collective-permute-done((bf16[4,32,256]{2,1,0:T(8,128)(2,1)S(1)}, bf16[4,32,256]{2,1,0:T(8,128)(2,1)S(1)}, u32[]{:S(2)}, u32[]{:S(2)}) %collective-permute-start.33) | collective-permute-done | bytes 65568 | tf_op jit(solution)/shard_map/while/body/eval_jaxpr/ppermute | solution.py:125
  346.4 3.9 %collective-permute-done.34 = bf16[4,32,256]{2,1,0:T(8,128)(2,1)S(1)} collective-permute-done((bf16[4,32,256]{2,1,0:T(8,128)(2,1)S(1)}, bf16[4,32,256]{2,1,0:T(8,128)(2,1)S(1)}, u32[]{:S(2)}, u32[]{:S(2)}) %collective-permute-start.34) | collective-permute-done | bytes 65568 | tf_op jit(solution)/shard_map/while/body/eval_jaxpr/ppermute | solution.py:125
  356.9 4.3 %collective-permute-done.36 = bf16[4,32,256]{2,1,0:T(8,128)(2,1)S(1)} collective-permute-done((bf16[4,32,256]{2,1,0:T(8,128)(2,1)S(1)}, bf16[4,32,256]{2,1,0:T(8,128)(2,1)S(1)}, u32[]{:S(2)}, u32[]{:S(2)}) %collective-permute-start.36) | collective-permute-done | bytes 65568 | tf_op jit(solution)/shard_map/while/body/eval_jaxpr/ppermute | solution.py:125
  (271 shorter events, 241.8 us)
Async XLA Ops:
  20.0 5.8 %collective-permute-start.3 = (bf16[4,32,256]{2,1,0:T(8,128)(2,1)S(1)}, bf16[4,32,256]{2,1,0:T(8,128)(2,1)S(1)}, u32[]{:S(2)}, u32[]{:S(2)}) collective-permute-start(bf16[4,32,256]{2,1,0:T(8,128)(2,1)S(1)} %broadcast_select_fusion.51), channel_id=1, source_target_pairs={{0,16},{2,18},{4,20},{6,22},{8,24},{10,26},{12,28},{14,30},{16,0},... | collective-permute-start | bytes 196616 | tf_op jit(solution)/shard_map/while/body/eval_jaxpr/ppermute | solution.py:125
  30.3 6.6 %collective-permute-start.5 = (bf16[4,32,256]{2,1,0:T(8,128)(2,1)S(1)}, bf16[4,32,256]{2,1,0:T(8,128)(2,1)S(1)}, u32[]{:S(2)}, u32[]{:S(2)}) collective-permute-start(bf16[4,32,256]{2,1,0:T(8,128)(2,1)S(1)} %broadcast_select_fusion.53), channel_id=1, source_target_pairs={{0,96},{2,98},{4,100},{6,102},{8,104},{10,106},{12,108},{14,110},{... | collective-permute-start | bytes 196616 | tf_op jit(solution)/shard_map/while/body/eval_jaxpr/ppermute | solution.py:125
  32.9 13.0 %collective-permute-start.7 = (bf16[4,32,256]{2,1,0:T(8,128)(2,1)S(1)}, bf16[4,32,256]{2,1,0:T(8,128)(2,1)S(1)}, u32[]{:S(2)}, u32[]{:S(2)}) collective-permute-start(bf16[4,32,256]{2,1,0:T(8,128)(2,1)S(1)} %get-tuple-element.364), channel_id=1, source_target_pairs={{2,4},{6,8},{10,12},{14,16},{18,20},{22,24},{26,28},{30,32},{34,36... | collective-permute-start | bytes 196616 | tf_op jit(solution)/shard_map/while/body/eval_jaxpr/ppermute | solution.py:161
  37.0 11.8 %collective-permute-start.6 = (bf16[4,32,256]{2,1,0:T(8,128)(2,1)S(1)}, bf16[4,32,256]{2,1,0:T(8,128)(2,1)S(1)}, u32[]{:S(2)}, u32[]{:S(2)}) collective-permute-start(bf16[4,32,256]{2,1,0:T(8,128)(2,1)S(1)} %broadcast_select_fusion.54), channel_id=1, source_target_pairs={{0,224},{2,226},{4,228},{6,230},{8,232},{10,234},{12,236},{14,238}... | collective-permute-start | bytes 196616 | tf_op jit(solution)/shard_map/while/body/eval_jaxpr/ppermute | solution.py:125
  56.2 6.2 %collective-permute-start.10 = (bf16[4,32,256]{2,1,0:T(8,128)(2,1)S(1)}, bf16[4,32,256]{2,1,0:T(8,128)(2,1)S(1)}, u32[]{:S(2)}, u32[]{:S(2)}) collective-permute-start(bf16[4,32,256]{2,1,0:T(8,128)(2,1)S(1)} %broadcast_select_fusion.55), channel_id=1, source_target_pairs={{0,12},{2,14},{4,8},{6,10},{8,4},{10,6},{12,0},{14,2},{16,28},{18,... | collective-permute-start | bytes 196616 | tf_op jit(solution)/shard_map/while/body/eval_jaxpr/ppermute | solution.py:125
  62.5 5.8 %collective-permute-start.11 = (bf16[4,32,256]{2,1,0:T(8,128)(2,1)S(1)}, bf16[4,32,256]{2,1,0:T(8,128)(2,1)S(1)}, u32[]{:S(2)}, u32[]{:S(2)}) collective-permute-start(bf16[4,32,256]{2,1,0:T(8,128)(2,1)S(1)} %broadcast_select_fusion.56), channel_id=1, source_target_pairs={{0,16},{2,18},{4,20},{6,22},{8,24},{10,26},{12,28},{14,30},{16,0},... | collective-permute-start | bytes 196616 | tf_op jit(solution)/shard_map/while/body/eval_jaxpr/ppermute | solution.py:125
  74.4 10.1 %collective-permute-start.15 = (bf16[4,32,256]{2,1,0:T(8,128)(2,1)S(1)}, bf16[4,32,256]{2,1,0:T(8,128)(2,1)S(1)}, u32[]{:S(2)}, u32[]{:S(2)}) collective-permute-start(bf16[4,32,256]{2,1,0:T(8,128)(2,1)S(1)} %get-tuple-element.368), channel_id=1, source_target_pairs={{2,4},{6,8},{10,12},{14,16},{18,20},{22,24},{26,28},{30,32},{34,36... | collective-permute-start | bytes 196616 | tf_op jit(solution)/shard_map/while/body/eval_jaxpr/ppermute | solution.py:161
  78.5 7.3 %collective-permute-start.14 = (bf16[4,32,256]{2,1,0:T(8,128)(2,1)S(1)}, bf16[4,32,256]{2,1,0:T(8,128)(2,1)S(1)}, u32[]{:S(2)}, u32[]{:S(2)}) collective-permute-start(bf16[4,32,256]{2,1,0:T(8,128)(2,1)S(1)} %broadcast_select_fusion.59), channel_id=1, source_target_pairs={{0,224},{2,226},{4,228},{6,230},{8,232},{10,234},{12,236},{14,238}... | collective-permute-start | bytes 196616 | tf_op jit(solution)/shard_map/while/body/eval_jaxpr/ppermute | solution.py:125
  98.1 5.8 %collective-permute-start.19 = (bf16[4,32,256]{2,1,0:T(8,128)(2,1)S(1)}, bf16[4,32,256]{2,1,0:T(8,128)(2,1)S(1)}, u32[]{:S(2)}, u32[]{:S(2)}) collective-permute-start(bf16[4,32,256]{2,1,0:T(8,128)(2,1)S(1)} %broadcast_select_fusion.61), channel_id=1, source_target_pairs={{0,16},{2,18},{4,20},{6,22},{8,24},{10,26},{12,28},{14,30},{16,0},... | collective-permute-start | bytes 196616 | tf_op jit(solution)/shard_map/while/body/eval_jaxpr/ppermute | solution.py:125
  110.0 10.1 %collective-permute-start.23 = (bf16[4,32,256]{2,1,0:T(8,128)(2,1)S(1)}, bf16[4,32,256]{2,1,0:T(8,128)(2,1)S(1)}, u32[]{:S(2)}, u32[]{:S(2)}) collective-permute-start(bf16[4,32,256]{2,1,0:T(8,128)(2,1)S(1)} %get-tuple-element.374), channel_id=1, source_target_pairs={{2,4},{6,8},{10,12},{14,16},{18,20},{22,24},{26,28},{30,32},{34,36... | collective-permute-start | bytes 196616 | tf_op jit(solution)/shard_map/while/body/eval_jaxpr/ppermute | solution.py:161
  114.0 7.3 %collective-permute-start.22 = (bf16[4,32,256]{2,1,0:T(8,128)(2,1)S(1)}, bf16[4,32,256]{2,1,0:T(8,128)(2,1)S(1)}, u32[]{:S(2)}, u32[]{:S(2)}) collective-permute-start(bf16[4,32,256]{2,1,0:T(8,128)(2,1)S(1)} %broadcast_select_fusion.64), channel_id=1, source_target_pairs={{0,224},{2,226},{4,228},{6,230},{8,232},{10,234},{12,236},{14,238}... | collective-permute-start | bytes 196616 | tf_op jit(solution)/shard_map/while/body/eval_jaxpr/ppermute | solution.py:125
  133.7 5.8 %collective-permute-start.27 = (bf16[4,32,256]{2,1,0:T(8,128)(2,1)S(1)}, bf16[4,32,256]{2,1,0:T(8,128)(2,1)S(1)}, u32[]{:S(2)}, u32[]{:S(2)}) collective-permute-start(bf16[4,32,256]{2,1,0:T(8,128)(2,1)S(1)} %broadcast_select_fusion.66), channel_id=1, source_target_pairs={{0,16},{2,18},{4,20},{6,22},{8,24},{10,26},{12,28},{14,30},{16,0},... | collective-permute-start | bytes 196616 | tf_op jit(solution)/shard_map/while/body/eval_jaxpr/ppermute | solution.py:125
  145.1 10.1 %collective-permute-start.31 = (bf16[4,32,256]{2,1,0:T(8,128)(2,1)S(1)}, bf16[4,32,256]{2,1,0:T(8,128)(2,1)S(1)}, u32[]{:S(2)}, u32[]{:S(2)}) collective-permute-start(bf16[4,32,256]{2,1,0:T(8,128)(2,1)S(1)} %get-tuple-element.380), channel_id=1, source_target_pairs={{2,4},{6,8},{10,12},{14,16},{18,20},{22,24},{26,28},{30,32},{34,36... | collective-permute-start | bytes 196616 | tf_op jit(solution)/shard_map/while/body/eval_jaxpr/ppermute | solution.py:161
  149.5 7.3 %collective-permute-start.30 = (bf16[4,32,256]{2,1,0:T(8,128)(2,1)S(1)}, bf16[4,32,256]{2,1,0:T(8,128)(2,1)S(1)}, u32[]{:S(2)}, u32[]{:S(2)}) collective-permute-start(bf16[4,32,256]{2,1,0:T(8,128)(2,1)S(1)} %broadcast_select_fusion.69), channel_id=1, source_target_pairs={{0,224},{2,226},{4,228},{6,230},{8,232},{10,234},{12,236},{14,238}... | collective-permute-start | bytes 196616 | tf_op jit(solution)/shard_map/while/body/eval_jaxpr/ppermute | solution.py:125
  169.2 5.8 %collective-permute-start.35 = (bf16[4,32,256]{2,1,0:T(8,128)(2,1)S(1)}, bf16[4,32,256]{2,1,0:T(8,128)(2,1)S(1)}, u32[]{:S(2)}, u32[]{:S(2)}) collective-permute-start(bf16[4,32,256]{2,1,0:T(8,128)(2,1)S(1)} %broadcast_select_fusion.71), channel_id=1, source_target_pairs={{0,16},{2,18},{4,20},{6,22},{8,24},{10,26},{12,28},{14,30},{16,0},... | collective-permute-start | bytes 196616 | tf_op jit(solution)/shard_map/while/body/eval_jaxpr/ppermute | solution.py:125
  180.4 10.1 %collective-permute-start.39 = (bf16[4,32,256]{2,1,0:T(8,128)(2,1)S(1)}, bf16[4,32,256]{2,1,0:T(8,128)(2,1)S(1)}, u32[]{:S(2)}, u32[]{:S(2)}) collective-permute-start(bf16[4,32,256]{2,1,0:T(8,128)(2,1)S(1)} %get-tuple-element.386), channel_id=1, source_target_pairs={{2,4},{6,8},{10,12},{14,16},{18,20},{22,24},{26,28},{30,32},{34,36... | collective-permute-start | bytes 196616 | tf_op jit(solution)/shard_map/while/body/eval_jaxpr/ppermute | solution.py:161
  185.2 7.6 %collective-permute-start.38 = (bf16[4,32,256]{2,1,0:T(8,128)(2,1)}, bf16[4,32,256]{2,1,0:T(8,128)(2,1)}, u32[]{:S(2)}, u32[]{:S(2)}) collective-permute-start(bf16[4,32,256]{2,1,0:T(8,128)(2,1)} %broadcast_select_fusion.74), channel_id=1, source_target_pairs={{0,224},{2,226},{4,228},{6,230},{8,232},{10,234},{12,236},{14,238}... | collective-permute-start | bytes 196616 | tf_op jit(solution)/shard_map/while/body/eval_jaxpr/ppermute | solution.py:125
  206.1 5.8 %collective-permute-start.3 = (bf16[4,32,256]{2,1,0:T(8,128)(2,1)S(1)}, bf16[4,32,256]{2,1,0:T(8,128)(2,1)S(1)}, u32[]{:S(2)}, u32[]{:S(2)}) collective-permute-start(bf16[4,32,256]{2,1,0:T(8,128)(2,1)S(1)} %broadcast_select_fusion.51), channel_id=1, source_target_pairs={{0,16},{2,18},{4,20},{6,22},{8,24},{10,26},{12,28},{14,30},{16,0},... | collective-permute-start | bytes 196616 | tf_op jit(solution)/shard_map/while/body/eval_jaxpr/ppermute | solution.py:125
  217.2 10.1 %collective-permute-start.7 = (bf16[4,32,256]{2,1,0:T(8,128)(2,1)S(1)}, bf16[4,32,256]{2,1,0:T(8,128)(2,1)S(1)}, u32[]{:S(2)}, u32[]{:S(2)}) collective-permute-start(bf16[4,32,256]{2,1,0:T(8,128)(2,1)S(1)} %get-tuple-element.364), channel_id=1, source_target_pairs={{2,4},{6,8},{10,12},{14,16},{18,20},{22,24},{26,28},{30,32},{34,36... | collective-permute-start | bytes 196616 | tf_op jit(solution)/shard_map/while/body/eval_jaxpr/ppermute | solution.py:161
  221.9 8.4 %collective-permute-start.6 = (bf16[4,32,256]{2,1,0:T(8,128)(2,1)S(1)}, bf16[4,32,256]{2,1,0:T(8,128)(2,1)S(1)}, u32[]{:S(2)}, u32[]{:S(2)}) collective-permute-start(bf16[4,32,256]{2,1,0:T(8,128)(2,1)S(1)} %broadcast_select_fusion.54), channel_id=1, source_target_pairs={{0,224},{2,226},{4,228},{6,230},{8,232},{10,234},{12,236},{14,238}... | collective-permute-start | bytes 196616 | tf_op jit(solution)/shard_map/while/body/eval_jaxpr/ppermute | solution.py:125
  243.2 5.8 %collective-permute-start.11 = (bf16[4,32,256]{2,1,0:T(8,128)(2,1)S(1)}, bf16[4,32,256]{2,1,0:T(8,128)(2,1)S(1)}, u32[]{:S(2)}, u32[]{:S(2)}) collective-permute-start(bf16[4,32,256]{2,1,0:T(8,128)(2,1)S(1)} %broadcast_select_fusion.56), channel_id=1, source_target_pairs={{0,16},{2,18},{4,20},{6,22},{8,24},{10,26},{12,28},{14,30},{16,0},... | collective-permute-start | bytes 196616 | tf_op jit(solution)/shard_map/while/body/eval_jaxpr/ppermute | solution.py:125
  255.5 10.1 %collective-permute-start.15 = (bf16[4,32,256]{2,1,0:T(8,128)(2,1)S(1)}, bf16[4,32,256]{2,1,0:T(8,128)(2,1)S(1)}, u32[]{:S(2)}, u32[]{:S(2)}) collective-permute-start(bf16[4,32,256]{2,1,0:T(8,128)(2,1)S(1)} %get-tuple-element.368), channel_id=1, source_target_pairs={{2,4},{6,8},{10,12},{14,16},{18,20},{22,24},{26,28},{30,32},{34,36... | collective-permute-start | bytes 196616 | tf_op jit(solution)/shard_map/while/body/eval_jaxpr/ppermute | solution.py:161
  258.5 8.0 %collective-permute-start.14 = (bf16[4,32,256]{2,1,0:T(8,128)(2,1)S(1)}, bf16[4,32,256]{2,1,0:T(8,128)(2,1)S(1)}, u32[]{:S(2)}, u32[]{:S(2)}) collective-permute-start(bf16[4,32,256]{2,1,0:T(8,128)(2,1)S(1)} %broadcast_select_fusion.59), channel_id=1, source_target_pairs={{0,224},{2,226},{4,228},{6,230},{8,232},{10,234},{12,236},{14,238}... | collective-permute-start | bytes 196616 | tf_op jit(solution)/shard_map/while/body/eval_jaxpr/ppermute | solution.py:125
  278.8 5.8 %collective-permute-start.19 = (bf16[4,32,256]{2,1,0:T(8,128)(2,1)S(1)}, bf16[4,32,256]{2,1,0:T(8,128)(2,1)S(1)}, u32[]{:S(2)}, u32[]{:S(2)}) collective-permute-start(bf16[4,32,256]{2,1,0:T(8,128)(2,1)S(1)} %broadcast_select_fusion.61), channel_id=1, source_target_pairs={{0,16},{2,18},{4,20},{6,22},{8,24},{10,26},{12,28},{14,30},{16,0},... | collective-permute-start | bytes 196616 | tf_op jit(solution)/shard_map/while/body/eval_jaxpr/ppermute | solution.py:125
  291.3 10.1 %collective-permute-start.23 = (bf16[4,32,256]{2,1,0:T(8,128)(2,1)S(1)}, bf16[4,32,256]{2,1,0:T(8,128)(2,1)S(1)}, u32[]{:S(2)}, u32[]{:S(2)}) collective-permute-start(bf16[4,32,256]{2,1,0:T(8,128)(2,1)S(1)} %get-tuple-element.374), channel_id=1, source_target_pairs={{2,4},{6,8},{10,12},{14,16},{18,20},{22,24},{26,28},{30,32},{34,36... | collective-permute-start | bytes 196616 | tf_op jit(solution)/shard_map/while/body/eval_jaxpr/ppermute | solution.py:161
  293.9 8.4 %collective-permute-start.22 = (bf16[4,32,256]{2,1,0:T(8,128)(2,1)S(1)}, bf16[4,32,256]{2,1,0:T(8,128)(2,1)S(1)}, u32[]{:S(2)}, u32[]{:S(2)}) collective-permute-start(bf16[4,32,256]{2,1,0:T(8,128)(2,1)S(1)} %broadcast_select_fusion.64), channel_id=1, source_target_pairs={{0,224},{2,226},{4,228},{6,230},{8,232},{10,234},{12,236},{14,238}... | collective-permute-start | bytes 196616 | tf_op jit(solution)/shard_map/while/body/eval_jaxpr/ppermute | solution.py:125
  314.7 5.8 %collective-permute-start.27 = (bf16[4,32,256]{2,1,0:T(8,128)(2,1)S(1)}, bf16[4,32,256]{2,1,0:T(8,128)(2,1)S(1)}, u32[]{:S(2)}, u32[]{:S(2)}) collective-permute-start(bf16[4,32,256]{2,1,0:T(8,128)(2,1)S(1)} %broadcast_select_fusion.66), channel_id=1, source_target_pairs={{0,16},{2,18},{4,20},{6,22},{8,24},{10,26},{12,28},{14,30},{16,0},... | collective-permute-start | bytes 196616 | tf_op jit(solution)/shard_map/while/body/eval_jaxpr/ppermute | solution.py:125
  326.2 10.1 %collective-permute-start.31 = (bf16[4,32,256]{2,1,0:T(8,128)(2,1)S(1)}, bf16[4,32,256]{2,1,0:T(8,128)(2,1)S(1)}, u32[]{:S(2)}, u32[]{:S(2)}) collective-permute-start(bf16[4,32,256]{2,1,0:T(8,128)(2,1)S(1)} %get-tuple-element.380), channel_id=1, source_target_pairs={{2,4},{6,8},{10,12},{14,16},{18,20},{22,24},{26,28},{30,32},{34,36... | collective-permute-start | bytes 196616 | tf_op jit(solution)/shard_map/while/body/eval_jaxpr/ppermute | solution.py:161
  330.6 7.4 %collective-permute-start.30 = (bf16[4,32,256]{2,1,0:T(8,128)(2,1)S(1)}, bf16[4,32,256]{2,1,0:T(8,128)(2,1)S(1)}, u32[]{:S(2)}, u32[]{:S(2)}) collective-permute-start(bf16[4,32,256]{2,1,0:T(8,128)(2,1)S(1)} %broadcast_select_fusion.69), channel_id=1, source_target_pairs={{0,224},{2,226},{4,228},{6,230},{8,232},{10,234},{12,236},{14,238}... | collective-permute-start | bytes 196616 | tf_op jit(solution)/shard_map/while/body/eval_jaxpr/ppermute | solution.py:125
  350.3 5.8 %collective-permute-start.35 = (bf16[4,32,256]{2,1,0:T(8,128)(2,1)S(1)}, bf16[4,32,256]{2,1,0:T(8,128)(2,1)S(1)}, u32[]{:S(2)}, u32[]{:S(2)}) collective-permute-start(bf16[4,32,256]{2,1,0:T(8,128)(2,1)S(1)} %broadcast_select_fusion.71), channel_id=1, source_target_pairs={{0,16},{2,18},{4,20},{6,22},{8,24},{10,26},{12,28},{14,30},{16,0},... | collective-permute-start | bytes 196616 | tf_op jit(solution)/shard_map/while/body/eval_jaxpr/ppermute | solution.py:125
  361.7 12.4 %collective-permute-start.39 = (bf16[4,32,256]{2,1,0:T(8,128)(2,1)S(1)}, bf16[4,32,256]{2,1,0:T(8,128)(2,1)S(1)}, u32[]{:S(2)}, u32[]{:S(2)}) collective-permute-start(bf16[4,32,256]{2,1,0:T(8,128)(2,1)S(1)} %get-tuple-element.386), channel_id=1, source_target_pairs={{2,4},{6,8},{10,12},{14,16},{18,20},{22,24},{26,28},{30,32},{34,36... | collective-permute-start | bytes 196616 | tf_op jit(solution)/shard_map/while/body/eval_jaxpr/ppermute | solution.py:161
  367.0 8.1 %collective-permute-start.38 = (bf16[4,32,256]{2,1,0:T(8,128)(2,1)}, bf16[4,32,256]{2,1,0:T(8,128)(2,1)}, u32[]{:S(2)}, u32[]{:S(2)}) collective-permute-start(bf16[4,32,256]{2,1,0:T(8,128)(2,1)} %broadcast_select_fusion.74), channel_id=1, source_target_pairs={{0,224},{2,226},{4,228},{6,230},{8,232},{10,234},{12,236},{14,238}... | collective-permute-start | bytes 196616 | tf_op jit(solution)/shard_map/while/body/eval_jaxpr/ppermute | solution.py:125
  (64 other events, 241.1 us)
